TPU v7x, 256 devices: a whole 4x4x8 slice. The times are simulated.
256 devices in a mesh: band: 8 (over z), gy: 32 (over x, y, core).
Axes of the slice: x: 4, y: 4, z: 8, core: 2. Of those that a mesh axis runs over, the one named last changes fastest.
Arguments:
- orbitals: float32 [32, 32, 512, 256], P('band', None, 'gy'), may hold values from -11 to 11
- potentials: float32 [2, 32, 512, 256], P(None, None, 'gy'), may hold values from -1 to 3
- local_potential: float32 [32, 512, 256], P(None, 'gy'), may hold values from 0 to 1
- shifts: float32 [32], P('band'), may hold values from 0.05 to 0.8
Outputs:
- field_response: float32 [2, 32, 256, 512], P(None, 'band', 'gy')
All inputs are finite; a program needn't handle non-finite values.
Results may differ from a plain program's by a relative error of at most 0.0003.
Values sent between devices are 32-bit elements; how exact they have to be, the bound alone decides.
A program may use at most 128 MiB of HBM per device.

v0:
```python
import jax
import jax.numpy as jnp
import numpy as np
from jax import lax
from jax.experimental import pallas as pl
from jax.experimental.pallas import tpu as pltpu
from jax.sharding import PartitionSpec as P

NX, NY, NZ, NPOT, SWEEPS, NORB = 256, 512, 32, 2, 3, 32
NB, NG = 8, 32
NL = NORB // NB
NR = NY // NG
NF = NL * NPOT
H = 3
KZ, KX = NZ // NB, NX // NG
PK = NPOT * KZ
T = 128
ZO = 8
ROWS = NR + 2 * H
ZB = ZO + NZ
SLAB = ROWS * 2 * ZB + ZO
PIECES = ((3, 3), (6, 3), (9, 4), (13, 3), (0, 3))
GROUP = 4
SPREAD, SCREEN = 3.5, 0.25
MESH = pl.DeviceIdType.MESH
f32, bf16 = jnp.float32, jnp.bfloat16


def sine(length):
    k = np.arange(1, length + 1, dtype=np.float64)
    return np.sqrt(2.0 / (length + 1)) * np.sin(np.pi * np.outer(k, k) / (length + 1))


def halves(table):
    high = table.astype(np.float32).astype(bf16)
    low = (table - high.astype(np.float64)).astype(np.float32).astype(bf16)
    return high, low


def tables():
    zh, zl = halves(sine(NZ))
    lz = np.zeros((NB, NPOT, KZ, NPOT, 3, NZ), bf16)
    for p in range(NPOT):
        for i, part in enumerate((zh, zh, zl)):
            lz[:, p, :, p, i, :] = part.reshape(NB, KZ, NZ)
    lz = lz.reshape(NB * PK, NPOT * 3 * NZ)
    sx = np.stack(halves(sine(NX)))
    sy = np.stack(halves(sine(NY)))
    st, y, j = np.meshgrid(np.arange(NG // 8), np.arange(NR), np.arange(8), indexing="ij")
    sy = sy[:, (NR * (8 * st + j) + y).reshape(-1), :]
    return lz, sx, sy


def split(value):
    high = value.astype(bf16)
    return high, (value - high.astype(f32)).astype(bf16)


def polynomial(shift):
    c = shift + SPREAD
    ratio = c / SPREAD
    now = 1.0 / ratio
    d, r, x = [1.0 / c], [jnp.ones_like(c)], []

    def add(a, b):
        out = []
        for i in range(max(len(a), len(b))):
            if i < len(a) and i < len(b):
                out.append(a[i] + b[i])
            else:
                out.append(a[i] if i < len(a) else b[i])
        return out

    for _ in range(SWEEPS):
        x = add(x, d)
        ad = [c * d[0]]
        for i in range(1, len(d)):
            ad.append(c * d[i] - 0.5 * d[i - 1])
        ad.append(-0.5 * d[-1])
        r = add(r, [-v for v in ad])
        after = 1.0 / (2.0 * ratio - now)
        d = add([after * now * v for v in d], [(2.0 * after / SPREAD) * v for v in r])
        now = after
    return add(x, d)


def kernel(
    orb_hbm, pot_hbm, loc_hbm, shift_ref, lz_hbm, sx_hbm, sy_hbm, out_ref,
    orbv, potv, locv, lz, sx, sy, f0, f1, f2, cf, pc, msg, rmsg,
    e0, e1, part, inbox, dv, ov, rv, wgt,
    load_sem, table_sem, hsend, hrecv, msend, mrecv, rsend, rrecv, asend, arecv,
):
    band, gy = lax.axis_index("band"), lax.axis_index("gy")

    barrier = pltpu.get_barrier_semaphore()
    for d in range(1, NG):
        pl.semaphore_signal(barrier, 1, device_id=(band, lax.rem(gy + d, NG)), device_id_type=MESH)
    for d in range(1, NB):
        pl.semaphore_signal(barrier, 1, device_id=(lax.rem(band + d, NB), gy), device_id_type=MESH)

    arrays = ((orb_hbm, orbv), (pot_hbm, potv), (loc_hbm, locv))
    for y in range(NR):
        for i, (src, dst) in enumerate(arrays):
            pltpu.make_async_copy(src.at[:, y], dst.at[H + y], load_sem.at[i, y // GROUP]).start()
    tables_in = []
    for i, (src, dst) in enumerate(((lz_hbm, lz), (sx_hbm, sx), (sy_hbm, sy))):
        tables_in.append(pltpu.make_async_copy(src, dst, table_sem.at[i]))
        tables_in[-1].start()

    zero = jnp.zeros((8, T), f32)

    def sums(r, acc):
        acc = list(acc)
        for z in range(NZ // 8):
            for x in range(2):
                cols = slice(T * x, T * (x + 1))
                pots = [potv[r, p * NZ + z * 8 : p * NZ + z * 8 + 8, cols] for p in range(NPOT)]
                for n in range(NL):
                    o = orbv[r, n * NZ + z * 8 : n * NZ + z * 8 + 8, cols]
                    q = o * o
                    for p in range(NPOT):
                        acc[p * NL + n] = acc[p * NL + n] + pots[p] * q
                    acc[NF + n] = acc[NF + n] + q
        return tuple(acc)

    acc = tuple(zero for _ in range(NF + NL))
    for g in range(NR // GROUP):
        rows = pl.ds(H + g * GROUP, GROUP)
        for i, (_, dst) in enumerate(arrays):
            pltpu.make_async_copy(dst.at[rows], dst.at[rows], load_sem.at[i, g]).wait()
        acc = lax.fori_loop(H + g * GROUP, H + (g + 1) * GROUP, sums, acc)
    lane1 = lax.broadcasted_iota(jnp.int32, (1, T), 1)
    row = jnp.zeros((1, T), f32)
    for i, a in enumerate(acc):
        total = jnp.sum(jnp.sum(a, axis=0, keepdims=True), axis=1, keepdims=True)
        row = jnp.where(lane1 == i, total, row)
    msg[...] = row

    pl.semaphore_wait(barrier, NG - 1 + NB - 1)

    for d in range(1, NG):
        pltpu.make_async_remote_copy(
            msg, rmsg.at[d], msend, mrecv,
            device_id=(band, lax.rem(gy + d, NG)), device_id_type=MESH,
        ).start()

    halo = []
    for side in range(2):
        target = lax.rem(gy + (NG - 1 if side == 0 else 1), NG)
        for i, (_, dst) in enumerate(arrays):
            width = H if i < 2 else H - 1
            if side == 0:
                src, to = pl.ds(H, width), pl.ds(H + NR, width)
            else:
                src, to = pl.ds(H + NR - width, width), pl.ds(H - width, width)
            copy = pltpu.make_async_remote_copy(
                dst.at[src], dst.at[to], hsend.at[side, i], hrecv.at[side, i],
                device_id=(band, target), device_id_type=MESH,
            )
            copy.start()
            halo.append(copy)

    def clear(i, carry):
        for f in range(NF):
            for field in (f0, f1, f2):
                field[f, pl.ds(pl.multiple_of(i * ZB, 8), ZO), :] = zero
        for n in range(NL):
            e0[n, pl.ds(pl.multiple_of(i * ZB, 8), ZO), :] = zero
        return carry

    lax.fori_loop(0, 2 * ROWS + 1, clear, 0)

    for n in range(NL):
        a = polynomial(jnp.full((8, T), shift_ref[n], f32))
        inverse = 1.0 / a[3]
        pc[n, 0] = a[2] * inverse
        pc[n, 1] = a[1] * inverse
        pc[n, 2] = a[0] * inverse
        pc[n, 3] = -4.0 * a[3]

    def index_of(shape, axis):
        return lax.broadcasted_iota(jnp.int32, shape, axis)

    shape = (PK * KX, NY)
    r_index = index_of(shape, 0)
    kz = band * KZ + lax.rem(lax.div(r_index, KX), KZ)
    kx = gy * KX + lax.rem(r_index, KX)
    qz = jnp.pi * (kz.astype(f32) + 1.0) / (NZ + 1)
    qx = jnp.pi * (kx.astype(f32) + 1.0) / (NX + 1)
    qy = jnp.pi * (index_of(shape, 1).astype(f32) + 1.0) / (NY + 1)
    wgt[...] = jnp.sqrt(4.0 * jnp.pi / (qz * qz + qx * qx + qy * qy + SCREEN))

    def whole(tile):
        return jnp.concatenate([tile] * (NZ // 8), axis=0)

    def at(r, x, shift=0):
        return pl.ds(pl.multiple_of((r * 2 + x) * ZB + ZO, 8) + shift, NZ)

    def half(ref, r, i, x):
        return ref[r, i * NZ : (i + 1) * NZ, x * T : (x + 1) * T]

    def w_of(r, x):
        return 1.0 - 2.0 * half(locv, r, 0, x)

    def source(r, mask=None):
        for x in range(2):
            pots = [half(potv, r, p, x) for p in range(NPOT)]
            for n in range(NL):
                o = half(orbv, r, n, x)
                if mask is not None:
                    o = o * mask
                for p in range(NPOT):
                    f = n * NPOT + p
                    f0[f, at(r, x), :] = (pots[p] - whole(cf[f])) * o

    lane = lax.broadcasted_iota(jnp.int32, (NZ, T), 1)
    first, last = lane == 0, lane == T - 1
    nought = jnp.zeros((NZ, T), f32)

    def near(field, f, r):
        c = [field[f, at(r, x), :] for x in range(2)]
        up = [pltpu.roll(v, 1, 1) for v in c]
        down = [pltpu.roll(v, T - 1, 1) for v in c]
        beside = [
            jnp.where(first, nought, up[0]) + jnp.where(last, down[1], down[0]),
            jnp.where(first, up[0], up[1]) + jnp.where(last, nought, down[1]),
        ]
        found = []
        for x in range(2):
            z = field[f, at(r, x, -1), :] + field[f, at(r, x, 1), :]
            y = field[f, at(r - 1, x), :] + field[f, at(r + 1, x), :]
            found.append(beside[x] + (z + y))
        return c, found

    def sweep_one(r, mask=None):
        w = [w_of(r, x) for x in range(2)]
        for n in range(NL):
            ws = [w[x] + whole(pc[n, 0]) for x in range(2)]
            for p in range(NPOT):
                f = n * NPOT + p
                c, s = near(f0, f, r)
                for x in range(2):
                    value = s[x] + ws[x] * c[x]
                    f1[f, at(r, x), :] = value if mask is None else value * mask

    def products(r):
        for x in range(2):
            pots = [half(potv, r, p, x) for p in range(NPOT)]
            for n in range(NL):
                o = half(orbv, r, n, x)
                e0[n, at(r, x), :] = o
                for p in range(NPOT):
                    f0[n * NPOT + p, at(r, x), :] = pots[p] * o

    def sweep_products(r):
        w = [w_of(r, x) for x in range(2)]
        for n in range(NL):
            ws = [w[x] + whole(pc[n, 0]) for x in range(2)]
            for src, dst, f in ((f0, f1, n * NPOT), (f0, f1, n * NPOT + 1), (e0, e1, n)):
                c, s = near(src, f, r)
                for x in range(2):
                    dst[f, at(r, x), :] = s[x] + ws[x] * c[x]

    def settle_source(r):
        for x in range(2):
            for n in range(NL):
                o = e0[n, at(r, x), :]
                for p in range(NPOT):
                    f = n * NPOT + p
                    f0[f, at(r, x), :] = f0[f, at(r, x), :] - whole(cf[f]) * o

    def settle_first(r):
        for x in range(2):
            for n in range(NL):
                o = e1[n, at(r, x), :]
                for p in range(NPOT):
                    f = n * NPOT + p
                    f1[f, at(r, x), :] = f1[f, at(r, x), :] - whole(cf[f]) * o

    def sweep_two(r, mask=None):
        w = [w_of(r, x) for x in range(2)]
        for n in range(NL):
            beta = whole(pc[n, 1])
            for p in range(NPOT):
                f = n * NPOT + p
                c, s = near(f1, f, r)
                for x in range(2):
                    value = s[x] + w[x] * c[x] + beta * f0[f, at(r, x), :]
                    f2[f, at(r, x), :] = value if mask is None else value * mask

    def last_sweep(r):
        w = [w_of(r, x) for x in range(2)]
        density = [[None, None] for _ in range(NPOT)]
        for n in range(NL):
            beta, gamma = whole(pc[n, 2]), whole(pc[n, 3])
            orbs = [half(orbv, r, n, x) * gamma for x in range(2)]
            for p in range(NPOT):
                f = n * NPOT + p
                c, s = near(f2, f, r)
                for x in range(2):
                    value = s[x] + w[x] * c[x] + beta * f0[f, at(r, x), :]
                    term = orbs[x] * value
                    old = density[p][x]
                    density[p][x] = term if old is None else old + term
        for x in range(2):
            stack = []
            for p in range(NPOT):
                high, low = split(density[p][x])
                stack += [high, low, high]
            along_z = jnp.dot(lz[...], jnp.concatenate(stack, axis=0), preferred_element_type=f32)
            for b in range(NB):
                part[b, r - H, :, T * x : T * (x + 1)] = along_z[b * PK : (b + 1) * PK, :]

    def send(k, way, kind):
        low, count = PIECES[k]
        far, reach = ((4, 2), (3, 1), (1, 1), (2, 2))[kind]
        rows = part_rows(k, way) if kind == 0 else pl.ds(low, count)
        chunk = lax.rem(band + (far if way == 0 else NB - far), NB)
        to = lax.rem(band + (reach if way == 0 else NB - reach), NB)
        return pltpu.make_async_remote_copy(
            part.at[chunk, rows], inbox.at[way, kind, rows], rsend.at[way, kind, k], rrecv.at[way, kind, k],
            device_id=(to, gy), device_id_type=MESH,
        )

    def part_rows(k, way):
        low, count = PIECES[k]
        cut = (count + (k % 2)) // 2
        return pl.ds(low, cut) if way == 0 else pl.ds(low + cut, count - cut)

    def begin(k):
        for kind in (0, 1, 2):
            for way in range(2):
                send(k, way, kind).start()

    def middle(k):
        low, count = PIECES[k]
        rows = pl.ds(low, count)
        for way in range(2):
            send(k, way, 0).wait_recv()
            send(k, way, 1).wait_recv()
            chunk = lax.rem(band + (2 if way == 0 else NB - 2), NB)
            part[chunk, rows] = part[chunk, rows] + inbox[way, 1, rows]
            some = part_rows(k, way)
            part[chunk, some] = part[chunk, some] + inbox[way, 0, some]
            send(k, way, 3).start()

    def finish(k):
        low, count = PIECES[k]
        rows = pl.ds(low, count)
        for kind in (2, 3):
            for way in range(2):
                send(k, way, kind).wait_recv()
        value = part[band, rows] + ((inbox[0, 2, rows] + inbox[1, 2, rows]) + (inbox[0, 3, rows] + inbox[1, 3, rows]))
        dv[low * PK : (low + count) * PK, :] = value.reshape(count * PK, NX)

    def loop(low, high, body):
        def step(r, carry):
            body(r)
            return carry

        if high == low + 1:
            body(low)
        else:
            lax.fori_loop(low, high, step, 0)

    loop(H, H + NR, products)
    loop(H + 1, H + NR - 1, sweep_products)

    pltpu.make_async_copy(rmsg.at[pl.ds(0, NG - 1)], rmsg.at[pl.ds(0, NG - 1)], mrecv).wait()
    total = msg[...]
    for d in range(1, NG):
        total = total + rmsg[d]
    for n in range(NL):
        norm = total[:, NF + n : NF + n + 1]
        for p in range(NPOT):
            value = total[:, p * NL + n : p * NL + n + 1] / norm
            cf[n * NPOT + p] = jnp.broadcast_to(value, (8, T))

    done = [H, H + 1, H + 2, H + 3]
    for k in range(3):
        end = H + PIECES[k][0] + PIECES[k][1]
        for i, body in enumerate((settle_source, settle_first, sweep_two, last_sweep)):
            stop = min(end + 3 - i, H + NR - i)
            loop(done[i], stop, body)
            done[i] = stop
            if k == 0 and i == 2:
                tables_in[0].wait()
        begin(k)
        if k > 0:
            middle(k - 1)

    low_mask = jnp.where(gy == 0, 0.0, 1.0).astype(f32)
    high_mask = jnp.where(gy == NG - 1, 0.0, 1.0).astype(f32)
    for copy in halo:
        copy.wait_recv()
    top = H + NR
    loop(top, top + 3, lambda r: source(r, high_mask))
    loop(top - 1, top, sweep_one)
    loop(top, top + 2, lambda r: sweep_one(r, high_mask))
    loop(top - 2, top, sweep_two)
    loop(top, top + 1, lambda r: sweep_two(r, high_mask))
    loop(top - 3, top, last_sweep)
    begin(3)
    middle(2)
    loop(0, H, lambda r: source(r, low_mask))
    loop(1, H, lambda r: sweep_one(r, low_mask))
    loop(H, H + 1, sweep_one)
    loop(H - 1, H, lambda r: sweep_two(r, low_mask))
    loop(H, H + 2, sweep_two)
    loop(H, H + 3, last_sweep)
    begin(4)
    middle(3)
    finish(0)
    finish(1)
    finish(2)
    middle(4)
    finish(3)
    finish(4)

    tables_in[1].wait()
    high, low = split(dv[...])

    def by_rows(a, b):
        return lax.dot_general(a, b, (((1,), (1,)), ((), ())), preferred_element_type=f32)

    along_x = by_rows(sx[0], high) + by_rows(sx[0], low) + by_rows(sx[1], high)
    ov[...] = along_x.reshape(NG, KX, NR * PK)

    for d in range(1, NG):
        target = lax.rem(gy + d, NG)
        pltpu.make_async_remote_copy(
            ov.at[target], rv.at[gy], asend, arecv, device_id=(band, target), device_id_type=MESH
        ).start()
    rv[gy] = ov[gy]
    tables_in[2].wait()

    others = pl.ds(0, NG - 1)
    pltpu.make_async_copy(rv.at[others], rv.at[others], arecv).wait()

    lane8 = lax.rem(lax.broadcasted_iota(jnp.int32, (KX, T), 1), 8)
    along_y = None
    for pair in range(NG // 16):
        columns = []
        for st in (2 * pair, 2 * pair + 1):
            tiles = [rv[st * 8 + j] for j in range(8)]
            column = []
            for pk in range(PK):
                got = None
                for j in range(8):
                    shift = (j - pk) % T
                    moved = tiles[j] if shift == 0 else pltpu.roll(tiles[j], shift, 1)
                    got = moved if got is None else jnp.where(lane8 == j, moved, got)
                column.append(got)
            columns.append(jnp.concatenate(column, axis=0))
        high, low = split(jnp.concatenate(columns, axis=1))
        k_rows = slice(pair * 2 * T, (pair + 1) * 2 * T)
        term = (
            jnp.dot(high, sy[0, k_rows], preferred_element_type=f32)
            + jnp.dot(low, sy[0, k_rows], preferred_element_type=f32)
            + jnp.dot(high, sy[1, k_rows], preferred_element_type=f32)
        )
        along_y = term if along_y is None else along_y + term
    out_ref[...] = along_y * wgt[...]

    for copy in halo:
        copy.wait_send()
    pltpu.make_async_copy(rmsg.at[pl.ds(0, NG - 1)], rmsg.at[pl.ds(0, NG - 1)], msend).wait()
    for k in range(len(PIECES)):
        for kind in range(4):
            for way in range(2):
                send(k, way, kind).wait_send()
    pltpu.make_async_copy(rv.at[others], rv.at[others], asend).wait()


def per_device(orbitals, potentials, local_potential, shifts):
    lz, sx, sy = tables()
    anywhere = pl.BlockSpec(memory_space=pl.ANY)
    field = pltpu.VMEM((NF, SLAB, T), f32)
    dma = pltpu.SemaphoreType.DMA
    out = pl.pallas_call(
        kernel,
        out_shape=jax.ShapeDtypeStruct((PK * KX, NY), f32),
        in_specs=[anywhere, anywhere, anywhere, pl.BlockSpec(memory_space=pltpu.SMEM)] + [anywhere] * 3,
        out_specs=pl.BlockSpec(memory_space=pltpu.VMEM),
        scratch_shapes=[
            pltpu.VMEM((ROWS, NL * NZ, NX), f32),
            pltpu.VMEM((ROWS, NPOT * NZ, NX), f32),
            pltpu.VMEM((ROWS, NZ, NX), f32),
            pltpu.VMEM((NB * PK, NPOT * 3 * NZ), bf16),
            pltpu.VMEM((2, NX, NX), bf16),
            pltpu.VMEM((2, NY, NY), bf16),
            field,
            field,
            field,
            pltpu.VMEM((NF, 8, T), f32),
            pltpu.VMEM((NL, 4, 8, T), f32),
            pltpu.VMEM((1, T), f32),
            pltpu.VMEM((NG, 1, T), f32),
            pltpu.VMEM((NL, SLAB, T), f32),
            pltpu.VMEM((NL, SLAB, T), f32),
            pltpu.VMEM((NB, NR, PK, NX), f32),
            pltpu.VMEM((2, 4, NR, PK, NX), f32),
            pltpu.VMEM((NR * PK, NX), f32),
            pltpu.VMEM((NG, KX, NR * PK), f32),
            pltpu.VMEM((NG, KX, NR * PK), f32),
            pltpu.VMEM((PK * KX, NY), f32),
            dma((3, NR // GROUP)),
            dma((3,)),
            dma((2, 3)),
            dma((2, 3)),
            dma,
            dma,
            dma((2, 4, len(PIECES))),
            dma((2, 4, len(PIECES))),
            dma,
            dma,
        ],
        compiler_params=pltpu.CompilerParams(
            collective_id=0, has_side_effects=True, vmem_limit_bytes=56 * 1024 * 1024
        ),
    )(
        orbitals.reshape(NL * NZ, NR, NX),
        potentials.reshape(NPOT * NZ, NR, NX),
        local_potential,
        shifts,
        jnp.asarray(lz),
        jnp.asarray(sx),
        jnp.asarray(sy),
    )
    return out.reshape(NPOT, KZ, KX, NY)


def solution(mesh):
    placed = (
        P("band", None, "gy", None),
        P(None, None, "gy", None),
        P(None, "gy", None),
        P("band"),
    )
    return jax.shard_map(
        per_device,
        mesh=mesh,
        in_specs=placed,
        out_specs=P(None, "band", "gy", None),
        check_vma=False,
    )
```

profile of v0, /device:TPU:1, one launch (start us, length us, event | category | flops | bytes accessed | tf_op | source)
XLA Modules:
  0.0 50.1 jit_solution(13868452342988250011)
XLA Ops:
  0.0 48.5 %shard_map.73 = f32[64,512]{1,0:T(8,128)} custom-call(f32[128,16,256]{2,1,0:T(8,128)} %bitcast.3, f32[64,16,256]{2,1,0:T(8,128)} %bitcast.4, f32[32,16,256]{2,1,0:T(8,128)} %loc_hbm.1, f32[4]{0:T(128)} %shift_ref.1, bf16[64,192]{1,0:T(8,128)(2,1)} %constant.6.clone.lz_hbm, bf16[2,256,256]{2,1,0:T(8,128)(2,1)} %constant.7.clone.sx_hbm, ...), custom_call_target="tpu_custom_call" | custom-call | tf_op jit(solution)/shard_map/pallas_call | solution.py:480
  48.5 1.6 %copy.9 = f32[2,4,8,512]{3,2,1,0:T(8,128)} copy(f32[2,4,8,512]{3,2,1,0:T(8,128)} %bitcast.5) | data formatting | bytes 262144
where the time goes:
time: 50.2 us; the launch traced here: 50.1 us
  Pallas kernels  48.5 us (97%)
  local copies, waits for them, and re-layouts  1.57 us (3%)
    pallas_call x1, Pallas kernels, per_device(): pl.pallas_call(kernel, out_shape=jax.ShapeDtypeStruct((PK * KX, NY), f32)...  48.5 us
    unnamed x1, local copies, waits for them, and re-layouts  1.57 us

commit v1 on v0

--- a/solution.py
+++ b/solution.py
@@ -385,9 +385,9 @@
             done[i] = stop
             if k == 0 and i == 2:
                 tables_in[0].wait()
+            if k == 2 and i == 2:
+                middle(0)
         begin(k)
-        if k > 0:
-            middle(k - 1)
 
     low_mask = jnp.where(gy == 0, 0.0, 1.0).astype(f32)
     high_mask = jnp.where(gy == NG - 1, 0.0, 1.0).astype(f32)
@@ -401,12 +401,13 @@
     loop(top, top + 1, lambda r: sweep_two(r, high_mask))
     loop(top - 3, top, last_sweep)
     begin(3)
-    middle(2)
+    middle(1)
     loop(0, H, lambda r: source(r, low_mask))
     loop(1, H, lambda r: sweep_one(r, low_mask))
     loop(H, H + 1, sweep_one)
     loop(H - 1, H, lambda r: sweep_two(r, low_mask))
     loop(H, H + 2, sweep_two)
+    middle(2)
     loop(H, H + 3, last_sweep)
     begin(4)
     middle(3)

time: 50.2 us -> 49.3 us (0.982)
  Pallas kernels: 48.5 us -> 47.6 us
    pallas_call x1, Pallas kernels: 48.5 us -> 47.6 us  [per_device(): pl.pallas_call(kernel, out_shape=jax.ShapeDtypeStruct((PK * KX, NY), f32)...]
where the time goes in v1:
time: 49.3 us; the launch traced here: 49.2 us
  Pallas kernels  47.6 us (97%)
  local copies, waits for them, and re-layouts  1.57 us (3%)
    pallas_call x1, Pallas kernels, per_device(): pl.pallas_call(kernel, out_shape=jax.ShapeDtypeStruct((PK * KX, NY), f32)...  47.6 us
    unnamed x1, local copies, waits for them, and re-layouts  1.57 us

profile of v1, /device:TPU:1, one launch (start us, length us, event | category | flops | bytes accessed | tf_op | source)
XLA Modules:
  0.0 49.2 jit_solution(9489143532284117426)
XLA Ops:
  0.0 47.6 %shard_map.73 = f32[64,512]{1,0:T(8,128)} custom-call(f32[128,16,256]{2,1,0:T(8,128)} %bitcast.3, f32[64,16,256]{2,1,0:T(8,128)} %bitcast.4, f32[32,16,256]{2,1,0:T(8,128)} %loc_hbm.1, f32[4]{0:T(128)} %shift_ref.1, bf16[64,192]{1,0:T(8,128)(2,1)} %constant.6.clone.lz_hbm, bf16[2,256,256]{2,1,0:T(8,128)(2,1)} %constant.7.clone.sx_hbm, ...), custom_call_target="tpu_custom_call" | custom-call | tf_op jit(solution)/shard_map/pallas_call | solution.py:481
  47.6 1.6 %copy.9 = f32[2,4,8,512]{3,2,1,0:T(8,128)} copy(f32[2,4,8,512]{3,2,1,0:T(8,128)} %bitcast.5) | data formatting | bytes 262144
